TPU v7x, 32 devices: a whole 2x2x4 slice. The times are simulated.
32 devices in a mesh: sect: 2 (over core), tok: 2 (over x), vocab: 8 (over z, y).
Axes of the slice: x: 2, y: 2, z: 4, core: 2. Of those that a mesh axis runs over, the one named last changes fastest.
Arguments:
- teacher_hidden: bfloat16 [512, 8192], P('tok', 'sect'), may hold values from -6 to 6
- teacher_head: bfloat16 [8192, 4096], P('sect', 'vocab'), may hold values from -0.19921875 to 0.19921875
- student_hidden: bfloat16 [512, 3072], P('tok', 'sect'), may hold values from -6 to 6
- student_head: bfloat16 [3072, 4096], P('sect', 'vocab'), may hold values from -0.328125 to 0.328125
- live_counts: int32 [2], P('tok'), may hold values from 1 to 256, 384 in all
Outputs:
- loss: float32 [], replicated
- head_grad: bfloat16 [3072, 4096], P(('sect', 'tok'), 'vocab')
- hidden_grad: bfloat16 [512, 3072], P(('tok', 'vocab'), 'sect')
Inputs may be any that keep to these rules, and one draw needn't show every extreme that they name: Shard k of the tokens has its first live_counts[k] token slots live and the rest empty.
All inputs are finite; a program needn't handle non-finite values.
Results may differ from a plain program's by a relative error of at most 0.0049.
Values may be sent and summed in bfloat16 or wider, within the bound.
A program may use at most 64 MiB of HBM per device.

v0:
```python
import jax
import jax.numpy as jnp
from jax import lax
from jax.sharding import PartitionSpec as P


def softened(teacher_logits, student_logits):
    teacher = teacher_logits * 0.5
    student = student_logits * 0.5
    teacher_exp = jnp.exp(teacher)
    student_exp = jnp.exp(student)
    partial_sums = (
        jnp.sum(teacher_exp, axis=1),
        jnp.sum(student_exp, axis=1),
        jnp.sum(teacher_exp * (teacher - student), axis=1),
    )
    return (teacher_exp, student_exp, partial_sums)


def finish(teacher_exp, student_exp, totals, live_rows, live_total, vocab_entries):
    teacher_sum, student_sum, cross = totals
    divergence = cross / teacher_sum - jnp.log(teacher_sum) + jnp.log(student_sum)
    numerator = jnp.sum(live_rows * divergence)
    row_scale = live_rows * (32.0 * vocab_entries * 0.5 / live_total)
    logit_grad = (
        row_scale[:, None]
        * (student_exp / student_sum[:, None] - teacher_exp / teacher_sum[:, None])
    ).astype(jnp.bfloat16)
    return (logit_grad, numerator)


def body(teacher_hidden, teacher_head, student_hidden, student_head, live_counts):
    token_rows = teacher_hidden.shape[0]
    vocab_entries = student_head.shape[1] * lax.axis_size("vocab")
    live_total = lax.psum(jnp.sum(live_counts.astype(jnp.float32)), "tok")
    live_rows = (jnp.arange(token_rows, dtype=jnp.int32) < live_counts[0]).astype(jnp.float32)
    teacher_part = jnp.dot(teacher_hidden, teacher_head, preferred_element_type=jnp.float32)
    student_part = jnp.dot(student_hidden, student_head, preferred_element_type=jnp.float32)
    teacher_logits, student_logits = lax.psum((teacher_part, student_part), "sect")
    teacher_exp, student_exp, partial_sums = softened(teacher_logits, student_logits)
    totals = lax.psum((partial_sums[0], partial_sums[1], partial_sums[2]), "vocab")
    logit_grad, numerator = finish(
        teacher_exp, student_exp, totals, live_rows, live_total, vocab_entries
    )
    owned_features = lax.all_to_all(student_hidden, "tok", split_axis=1, concat_axis=0, tiled=True)
    head_sum = lax.dot_general(
        owned_features,
        lax.all_gather(logit_grad, "tok", axis=0, tiled=True),
        (((0,), (0,)), ((), ())),
        preferred_element_type=jnp.float32,
    )
    head_grad = head_sum.astype(jnp.bfloat16)
    hidden_grad = lax.psum_scatter(
        lax.dot_general(
            logit_grad, student_head, (((1,), (1,)), ((), ())), preferred_element_type=jnp.float32
        ),
        "vocab",
        scatter_dimension=0,
        tiled=True,
    ).astype(jnp.bfloat16)
    loss = lax.psum(numerator, "tok") / live_total
    return (loss, head_grad, hidden_grad)


def solution(mesh):
    placed = (P("tok", "sect"), P("sect", "vocab"), P("tok", "sect"), P("sect", "vocab"), P("tok"))
    return jax.shard_map(
        body,
        mesh=mesh,
        in_specs=placed,
        out_specs=(P(), P(("sect", "tok"), "vocab"), P(("tok", "vocab"), "sect")),
        check_vma=False,
    )
```

profile of v0, /device:TPU:0, one launch (start us, length us, event | category | flops | bytes accessed | tf_op | source)
XLA Modules:
  0.0 144.1 jit_solution(9674600153131628786)
XLA Ops:
  7.2 0.0 copy-start
  7.2 0.0 copy-start.2
  7.2 0.0 all-reduce.5.cloned.1.call-start
  7.2 1.5 %copy-done = bf16[256,4096]{1,0:T(8,128)(2,1)S(1)} copy-done((bf16[256,4096]{1,0:T(8,128)(2,1)S(1)}, bf16[256,4096]{1,0:T(8,128)(2,1)}, u32[]{:S(2)}) %copy-start) | copy-done | bytes 2097176
  8.8 0.0 copy-start.1
  8.8 4.3 %fusion.3 = f32[256,512]{1,0:T(8,128)} fusion(bf16[256,4096]{1,0:T(8,128)(2,1)S(1)} %copy-done, bf16[4096,512]{1,0:T(8,128)(2,1)} %param.6), kind=kOutput, calls=%fused_computation.10 | convolution fusion | flops 1073741824 | bytes 6815744 | tf_op jit(solution)/shard_map/dot_general | solution.py:37
  13.1 0.0 copy-done.2
  13.1 0.0 copy-done.1
  13.1 1.4 fusion.4
  14.5 0.0 all-reduce.5.cloned.1.call-update
  14.5 0.0 reduce-scatter.2.cloned.1.call-start
  15.2 21.8 %all-reduce.5.cloned.1.call-done = (f32[256,512]{1,0:T(8,128)}, f32[256,512]{1,0:T(8,128)}) async-done(((f32[256,512]{1,0:T(8,128)}, f32[256,512]{1,0:T(8,128)}), (f32[256,512]{1,0:T(8,128)}, f32[256,512]{1,0:T(8,128)})) %all-reduce.5.cloned.1.call-update) | async-done | bytes 1048592 | tf_op jit(solution)/shard_map/psum | solution.py:39
  37.0 1.5 %multiply_reduce_fusion = (f32[256]{0:T(256)S(1)}, f32[256]{0:T(256)S(1)}, f32[256]{0:T(256)S(1)}) fusion(f32[256,512]{1,0:T(8,128)} %get-tuple-element.20, f32[256,512]{1,0:T(8,128)} %get-tuple-element.21), kind=kLoop, calls=%fused_computation.3 | loop fusion | flops 916736 | bytes 1051648 | tf_op jit(solution)/shard_map/reduce_sum | solution.py:15
  38.6 21.6 %all-reduce = (f32[256]{0:T(256)S(1)}, f32[256]{0:T(256)S(1)}, f32[256]{0:T(256)S(1)}) all-reduce(f32[256]{0:T(256)S(1)} %get-tuple-element.13, f32[256]{0:T(256)S(1)} %get-tuple-element.14, f32[256]{0:T(256)S(1)} %get-tuple-element.12), channel_id=1, replica_groups=mesh['sect'=2,'tok'=2,'vocab'=8] {'vocab'}, use_global_device_ids=true, to_apply=%region_7.0 | all-reduce | flops 768 | bytes 6144 | tf_op jit(solution)/shard_map/psum | solution.py:41
  60.2 0.6 select_reduce_fusion
  60.8 6.2 %all-reduce.1 = (f32[]{:T(128)}, f32[]{:T(128)}) all-reduce(f32[]{:T(128)} %select_reduce_fusion, f32[]{:T(128)} %bitcast.1), channel_id=1, replica_groups=mesh['sect'=2,'tok'=2,'vocab'=8] {'tok'}, use_global_device_ids=true, to_apply=%region_9.0 | all-reduce | flops 2 | bytes 16 | tf_op jit(solution)/shard_map/psum | solution.py:61
  67.7 1.4 multiply_convert_fusion
  69.1 3.2 %fusion.5 = f32[256,1536]{1,0:T(8,128)} fusion(bf16[256,512]{1,0:T(8,128)(2,1)S(1)} %multiply_convert_fusion, bf16[1536,512]{1,0:T(8,128)(2,1)} %param.8), kind=kOutput, calls=%fused_computation.12 | convolution fusion | flops 402653184 | bytes 3407872 | tf_op jit(solution)/shard_map/dot_general | solution.py:54
  72.3 0.0 reduce-scatter.2.cloned.1.call-update
  72.3 1.2 copy.10
  73.4 11.5 %all_to_all.19 = bf16[256,2,768]{0,2,1:T(8,128)(2,1)S(1)} all-to-all(bf16[256,2,768]{0,2,1:T(8,128)(2,1)} %bitcast.18), channel_id=1, replica_groups=mesh['sect'=2,'tok'=2,'vocab'=8] {'tok'}, dimensions={1} | all-to-all | bytes 1572864 | tf_op jit(solution)/shard_map/all_to_all | solution.py:45
  84.9 1.2 copy.11
  87.4 7.0 %all_gather.3 = bf16[512,512]{1,0:T(8,128)(2,1)S(1)} all-gather(bf16[256,512]{1,0:T(8,128)(2,1)S(1)} %multiply_convert_fusion), channel_id=1, replica_groups=mesh['sect'=2,'tok'=2,'vocab'=8] {'tok'}, dimensions={0}, use_global_device_ids=true | all-gather | bytes 786432 | tf_op jit(solution)/shard_map/all_gather | solution.py:48
  94.5 1.7 %fusion = bf16[768,512]{0,1:T(8,128)(2,1)S(1)} fusion(bf16[512,512]{1,0:T(8,128)(2,1)S(1)} %all_gather.3, bf16[512,768]{1,0:T(8,128)(2,1)} %bitcast.19), kind=kOutput, calls=%fused_computation.1 | convolution fusion | flops 403046400 | bytes 2097152 | tf_op jit(solution)/shard_map/dot_general | solution.py:46
  96.2 1.2 copy.12
  97.4 37.2 %reduce-scatter.2.cloned.1.call-done = f32[32,1536]{1,0:T(8,128)} async-done(((f32[256,1536]{1,0:T(8,128)}), f32[32,1536]{1,0:T(8,128)}) %reduce-scatter.2.cloned.1.call-update) | async-done | bytes 196624 | tf_op jit(solution)/shard_map/reduce_scatter | solution.py:53
  134.5 1.6 %convert_element_type.20 = bf16[32,1536]{1,0:T(8,128)(2,1)} convert(f32[32,1536]{1,0:T(8,128)} %reduce-scatter.2.cloned.1.call-done) | non-fusion elementwise | flops 49152 | bytes 294912 | tf_op jit(solution)/shard_map/convert_element_type | solution.py:60
  (1 shorter events, 0.0 us)
Async XLA Ops:
  7.2 1.6 %copy-start = (bf16[256,4096]{1,0:T(8,128)(2,1)S(1)}, bf16[256,4096]{1,0:T(8,128)(2,1)}, u32[]{:S(2)}) copy-start(bf16[256,4096]{1,0:T(8,128)(2,1)} %param.5) | copy-start | bytes 6291460
  7.2 5.9 %copy-start.2 = (bf16[256,1536]{1,0:T(8,128)(2,1)S(1)}, bf16[256,1536]{1,0:T(8,128)(2,1)}, u32[]{:S(2)}) copy-start(bf16[256,1536]{1,0:T(8,128)(2,1)} %param.7) | copy-start | bytes 2359300
  7.2 29.9 %all-reduce.5.cloned.1.call-start = ((), (), s32[]{:S(2)}) async-start(), calls=%async_computation.3 | async-start | bytes 2097152 | tf_op jit(solution)/shard_map/psum | solution.py:39
  8.8 4.4 %copy-start.1 = (bf16[1536,512]{1,0:T(8,128)(2,1)S(1)}, bf16[1536,512]{1,0:T(8,128)(2,1)}, u32[]{:S(2)}) copy-start(bf16[1536,512]{1,0:T(8,128)(2,1)} %param.8) | copy-start | bytes 4718596
  14.5 120.0 %reduce-scatter.2.cloned.1.call-start = ((), (), s32[]{:S(2)}) async-start(), calls=%async_computation.2 | async-start | bytes 1769472 | tf_op jit(solution)/shard_map/reduce_scatter | solution.py:53
Sparse Core Ops, SparseCore 0:
  14.7 22.3 all-reduce.4
  72.4 62.0 reduce-scatter.1
where the time goes:
time: 145 us; the launch traced here: 144 us
  waiting for transfers between devices  59 us (41%)
  blocking collectives  46.3 us (32%)
  between operations  17.9 us (12%)
  matrix products  10.6 us (7%)
  other arithmetic  5.12 us (4%)
  local copies, waits for them, and re-layouts  5.01 us (3%)
    reduce_scatter x1, waiting for transfers between devices, body(): lax.psum_scatter(lax.dot_general(logit_grad, student_head, (((1,), (1,)),...  37.2 us
    psum x1, waiting for transfers between devices, body(): lax.psum((teacher_part, student_part), 'sect')  21.8 us
    psum x1, blocking collectives, body(): lax.psum((partial_sums[0], partial_sums[1], partial_sums[2]), 'vocab')  21.6 us
    all_to_all x1, blocking collectives, body(): lax.all_to_all(student_hidden, 'tok', split_axis=1, concat_axis=0, tiled=...  11.5 us
    all_gather x1, blocking collectives, body(): lax.all_gather(logit_grad, 'tok', axis=0, tiled=True)  7.05 us
    psum x1, blocking collectives, body(): loss = lax.psum(numerator, 'tok') / live_total  6.16 us
    dot_general x1, matrix products, body(): jnp.dot(teacher_hidden, teacher_head, preferred_element_type=jnp.float32)  4.34 us
    unnamed x8, local copies, waits for them, and re-layouts  3.86 us
  transfers between devices with their start and end apart: 2, of which 2 were waited for; matrix products, arithmetic and copies ran while one was open for 4% of the time, Pallas kernels for 0%

commit v1 on v0

--- a/solution.py
+++ b/solution.py
@@ -1,6 +1,10 @@
+import functools
+
 import jax
 import jax.numpy as jnp
 from jax import lax
+from jax.experimental import pallas as pl
+from jax.experimental.pallas import tpu as pltpu
 from jax.sharding import PartitionSpec as P
 
 
@@ -62,10 +66,221 @@
     return (loss, head_grad, hidden_grad)
 
 
+MESH = pl.DeviceIdType.MESH
+TILE = 32
+F32, BF16 = jnp.float32, jnp.bfloat16
+
+
+def fused(
+    n_tok, n_voc, cw, fw,
+    counts, th_hbm, thead_hbm, sh_hbm, shead_hbm,
+    loss_ref, head_ref, hid_ref,
+    th, thead, sh, shead, part, precv, te_ref, se_ref, stat, ssend, srecv,
+    cnt, crecv, num, nrecv, hown, hrecv, grad, grecv, hs, hrv,
+    load_sem, p_ss, p_rs, c_ss, c_rs, h_ss, h_rs, s_ss, s_rs, g_ss, g_rs, n_ss, n_rs, d_ss, d_rs,
+):
+    sect, tok, voc = lax.axis_index("sect"), lax.axis_index("tok"), lax.axis_index("vocab")
+    rows, feats, width = sh.shape[0], sh.shape[1], shead.shape[1]
+    block, out_rows = feats // n_tok, rows // n_voc
+    chunks, f_chunks, tiles = width // cw, feats // fw, rows // TILE
+    other = {"sect": 1 - sect}
+    tok_peers = [(tok + d) % n_tok for d in range(1, n_tok)]
+    voc_peers = [(voc + d) % n_voc for d in range(1, n_voc)]
+
+    barrier = pltpu.get_barrier_semaphore()
+    pl.semaphore_signal(barrier, inc=1, device_id=other, device_id_type=MESH)
+    for p in tok_peers:
+        pl.semaphore_signal(barrier, inc=1, device_id={"tok": p}, device_id_type=MESH)
+    for p in voc_peers:
+        pl.semaphore_signal(barrier, inc=1, device_id={"vocab": p}, device_id_type=MESH)
+
+    loads = [
+        pltpu.make_async_copy(sh_hbm, sh, load_sem.at[0]),
+        pltpu.make_async_copy(shead_hbm, shead, load_sem.at[1]),
+        pltpu.make_async_copy(th_hbm, th, load_sem.at[2]),
+    ] + [
+        pltpu.make_async_copy(
+            thead_hbm.at[:, pl.ds(c * cw, cw)], thead.at[c], load_sem.at[3 + c]
+        )
+        for c in range(chunks)
+    ]
+    for load in loads:
+        load.start()
+
+    def send(src, dst, ss, rs, to):
+        copy = pltpu.make_async_remote_copy(
+            src_ref=src, dst_ref=dst, send_sem=ss, recv_sem=rs, device_id=to, device_id_type=MESH
+        )
+        copy.start()
+        return copy
+
+    cnt[...] = jnp.full(cnt.shape, counts[0].astype(F32))
+    loads[0].wait()
+    loads[1].wait()
+    pl.semaphore_wait(barrier, n_tok + n_voc - 1)
+    c_cp, h_cp, p_cp = [], [], []
+    for i, p in enumerate(tok_peers):
+        c_cp.append(send(cnt, crecv.at[i], c_ss.at[i], c_rs.at[i], {"tok": p}))
+        cols = pl.ds(pl.multiple_of(p * block, block), block)
+        h_cp.append(send(sh.at[:, cols], hrecv.at[i], h_ss.at[i], h_rs.at[i], {"tok": p}))
+    for c in range(chunks):
+        part[c] = jnp.dot(sh[...], shead[:, c * cw:(c + 1) * cw], preferred_element_type=F32)
+        p_cp.append(send(part.at[c], precv.at[c], p_ss.at[c], p_rs.at[c], other))
+    loads[2].wait()
+    for c in range(chunks):
+        loads[3 + c].wait()
+        q = chunks + c
+        part[q] = jnp.dot(th[...], thead[c], preferred_element_type=F32)
+        p_cp.append(send(part.at[q], precv.at[q], p_ss.at[q], p_rs.at[q], other))
+    hown[...] = sh[:, pl.ds(pl.multiple_of(tok * block, block), block)].T
+    for copy in p_cp:
+        copy.wait_recv()
+
+    lane = lax.broadcasted_iota(jnp.int32, (TILE, 128), 1)
+
+    def soften(i, carry):
+        at = pl.ds(pl.multiple_of(i * TILE, TILE), TILE)
+        zt = zs = cross = jnp.zeros((TILE, 1), F32)
+        for c in range(chunks):
+            s = (part[c, at, :] + precv[c, at, :]) * 0.5
+            t = (part[chunks + c, at, :] + precv[chunks + c, at, :]) * 0.5
+            te, se = jnp.exp(t), jnp.exp(s)
+            te_ref[c, at, :] = te
+            se_ref[c, at, :] = se
+            zt += jnp.sum(te, axis=1, keepdims=True)
+            zs += jnp.sum(se, axis=1, keepdims=True)
+            cross += jnp.sum(te * (t - s), axis=1, keepdims=True)
+        stat[at, :] = jnp.where(lane == 0, zt, jnp.where(lane == 1, zs, cross))
+        return carry
+
+    lax.fori_loop(0, tiles, soften, 0)
+    ssend[...] = stat[...].T[:8]
+    s_cp = [
+        send(ssend, srecv.at[i], s_ss.at[i], s_rs.at[i], {"vocab": p})
+        for i, p in enumerate(voc_peers)
+    ]
+    for copy in c_cp:
+        copy.wait_recv()
+    total = cnt[...]
+    for i in range(n_tok - 1):
+        total = total + crecv[i]
+    live_total = total[0:1, 0:1]
+    scale = 32.0 * (width * n_voc) * 0.5 / live_total
+    mine = cnt[0:1, 0:1]
+    totals = ssend[...]
+    for i, copy in enumerate(s_cp):
+        copy.wait_recv()
+        totals = totals + srecv[i]
+    stat[...] = jnp.concatenate([totals] * 16, axis=0).T
+
+    def finish_tile(i, acc):
+        at = pl.ds(pl.multiple_of(i * TILE, TILE), TILE)
+        sums = stat[at, :]
+        zt, zs, cross = sums[:, 0:1], sums[:, 1:2], sums[:, 2:3]
+        row = (lax.broadcasted_iota(jnp.int32, (TILE, 1), 0) + i * TILE).astype(F32)
+        live = (row < mine).astype(F32)
+        kl = cross / zt - jnp.log(zt) + jnp.log(zs)
+        a, b = live * scale / zs, live * scale / zt
+        for c in range(chunks):
+            g = a * se_ref[c, at, :] - b * te_ref[c, at, :]
+            grad[at, c * cw:(c + 1) * cw] = g.astype(BF16)
+        return acc + live * kl
+
+    acc = lax.fori_loop(0, tiles, finish_tile, jnp.zeros((TILE, 1), F32))
+    num[...] = jnp.broadcast_to(jnp.sum(acc, axis=0, keepdims=True), num.shape)
+    g_cp, n_cp, d_cp = [], [], []
+    for i, p in enumerate(tok_peers):
+        n_cp.append(send(num, nrecv.at[i], n_ss.at[i], n_rs.at[i], {"tok": p}))
+        g_cp.append(send(grad, grecv.at[i], g_ss.at[i], g_rs.at[i], {"tok": p}))
+    for f in range(f_chunks):
+        hs[f] = lax.dot_general(
+            grad[...], shead[f * fw:(f + 1) * fw, :], (((1,), (1,)), ((), ())),
+            preferred_element_type=F32,
+        ).astype(BF16)
+        for i, p in enumerate(voc_peers):
+            at = pl.ds(pl.multiple_of(p * out_rows, out_rows), out_rows)
+            d_cp.append(
+                (f, i, send(hs.at[f, at, :], hrv.at[i, f], d_ss.at[i, f], d_rs.at[i, f], {"vocab": p}))
+            )
+
+    head = jnp.dot(hown[...], grad[...], preferred_element_type=F32)
+    numerator = num[...]
+    for i in range(n_tok - 1):
+        h_cp[i].wait_recv()
+        n_cp[i].wait_recv()
+        numerator = numerator + nrecv[i]
+        theirs = hrecv[i].T
+        g_cp[i].wait_recv()
+        head = head + jnp.dot(theirs, grecv[i], preferred_element_type=F32)
+    head_ref[...] = head.astype(BF16)
+    loss_ref[...] = numerator / live_total
+
+    here = pl.ds(pl.multiple_of(voc * out_rows, out_rows), out_rows)
+    for f in range(f_chunks):
+        hid = hs[f, here, :].astype(F32)
+        for g, i, copy in d_cp:
+            if g == f:
+                copy.wait_recv()
+                hid = hid + hrv[i, f].astype(F32)
+        hid_ref[:, f * fw:(f + 1) * fw] = hid.astype(BF16)
+    for copy in p_cp + c_cp + h_cp + s_cp + g_cp + n_cp:
+        copy.wait_send()
+    for _, _, copy in d_cp:
+        copy.wait_send()
+
+
+def fused_body(n_tok, n_voc, teacher_hidden, teacher_head, student_hidden, student_head, live_counts):
+    rows, t_feats = teacher_hidden.shape
+    feats, width = student_head.shape
+    cw, fw = width // 2, feats // 3
+    block, out_rows = feats // n_tok, rows // n_voc
+    tp, vp, nf = n_tok - 1, n_voc - 1, feats // fw
+    vmem, dma = pltpu.VMEM, pltpu.SemaphoreType.DMA
+    any_spec = pl.BlockSpec(memory_space=pl.ANY)
+    vm_spec = pl.BlockSpec(memory_space=pltpu.VMEM)
+    loss, head, hid = pl.pallas_call(
+        functools.partial(fused, n_tok, n_voc, cw, fw),
+        out_shape=(
+            jax.ShapeDtypeStruct((8, 128), F32),
+            jax.ShapeDtypeStruct((block, width), BF16),
+            jax.ShapeDtypeStruct((out_rows, feats), BF16),
+        ),
+        in_specs=[pl.BlockSpec(memory_space=pltpu.SMEM)] + [any_spec] * 4,
+        out_specs=(vm_spec,) * 3,
+        scratch_shapes=[
+            vmem((rows, t_feats), BF16), vmem((2, t_feats, cw), BF16),
+            vmem((rows, feats), BF16), vmem((feats, width), BF16),
+            vmem((4, rows, cw), F32), vmem((4, rows, cw), F32),
+            vmem((2, rows, cw), F32), vmem((2, rows, cw), F32),
+            vmem((rows, 128), F32), vmem((8, rows), F32), vmem((vp, 8, rows), F32),
+            vmem((8, 128), F32), vmem((tp, 8, 128), F32),
+            vmem((8, 128), F32), vmem((tp, 8, 128), F32),
+            vmem((block, rows), BF16), vmem((tp, rows, block), BF16),
+            vmem((rows, width), BF16), vmem((tp, rows, width), BF16),
+            vmem((nf, rows, fw), BF16), vmem((vp, nf, out_rows, fw), BF16),
+            dma((5,)), dma((4,)), dma((4,)), dma((tp,)), dma((tp,)), dma((tp,)), dma((tp,)),
+            dma((vp,)), dma((vp,)), dma((tp,)), dma((tp,)), dma((tp,)), dma((tp,)),
+            dma((vp, nf)), dma((vp, nf)),
+        ],
+        compiler_params=pltpu.CompilerParams(
+            collective_id=0, has_side_effects=True, vmem_limit_bytes=48 * 1024 * 1024
+        ),
+    )(live_counts, teacher_hidden, teacher_head, student_hidden, student_head)
+    return (loss[0, 0], head, hid)
+
+
 def solution(mesh):
     placed = (P("tok", "sect"), P("sect", "vocab"), P("tok", "sect"), P("sect", "vocab"), P("tok"))
+    n_tok, n_voc = mesh.shape["tok"], mesh.shape["vocab"]
+
+    def run(*args):
+        rows = args[0].shape[0]
+        if rows % (TILE * n_voc) == 0 and n_tok > 1:
+            return fused_body(n_tok, n_voc, *args)
+        return body(*args)
+
     return jax.shard_map(
-        body,
+        run,
         mesh=mesh,
         in_specs=placed,
         out_specs=(P(), P(("sect", "tok"), "vocab"), P(("tok", "vocab"), "sect")),

time: 145 us -> 43.5 us (0.30)
  waiting for transfers between devices: 59 us -> 0 us
  blocking collectives: 46.3 us -> 0 us
  Pallas kernels: 0 us -> 35.8 us
  between operations: 17.9 us -> 1.3 us
  matrix products: 10.6 us -> 0 us
  other arithmetic: 5.12 us -> 0 us
    reduce_scatter x1 -> x0, waiting for transfers between devices: 37.2 us -> none  [body(): lax.psum_scatter(lax.dot_general(logit_grad, student_head, (((1,), (1,)),...]
    pallas_call x0 -> x1, Pallas kernels: none -> 35.8 us  [fused_body(): pl.pallas_call(functools.partial(fused, n_tok, n_voc, cw, fw), out_shape=...]
    psum x2 -> x0, blocking collectives: 27.8 us -> none  [the longest x1 21.6 us: body(): lax.psum((partial_sums[0], partial_sums[1], partial_sums[2]), 'vocab')]
    psum x1 -> x0, waiting for transfers between devices: 21.8 us -> none  [body(): lax.psum((teacher_part, student_part), 'sect')]
    all_to_all x1 -> x0, blocking collectives: 11.5 us -> none  [body(): lax.all_to_all(student_hidden, 'tok', split_axis=1, concat_axis=0, tiled=...]
    dot_general x4 -> x0, matrix products: 10.6 us -> none  [the longest x1 4.34 us: body(): jnp.dot(teacher_hidden, teacher_head, preferred_element_type=jnp.float32)]
    all_gather x1 -> x0, blocking collectives: 7.05 us -> none  [body(): lax.all_gather(logit_grad, 'tok', axis=0, tiled=True)]
    convert_element_type x2 -> x0, other arithmetic: 3 us -> none  [the longest x1 1.58 us: body(): hidden_grad = lax.psum_scatter(lax.dot_general(logit_grad, student_head,...]
  transfers between devices with their start and end apart: 2 -> 0, of which waited for: 2 -> 0; matrix products, arithmetic and copies ran while one was open for 4% -> 0% of each run, Pallas kernels for 0% -> 0%
where the time goes in v1:
time: 43.5 us; the launch traced here: 43.2 us
  Pallas kernels  35.8 us (82%)
  local copies, waits for them, and re-layouts  6.16 us (14%)
  between operations  1.3 us (3%)
    pallas_call x1, Pallas kernels, fused_body(): pl.pallas_call(functools.partial(fused, n_tok, n_voc, cw, fw), out_shape=...  35.8 us
    unnamed x8, local copies, waits for them, and re-layouts  5.64 us

profile of v1, /device:TPU:0, one launch (start us, length us, event | category | flops | bytes accessed | tf_op | source)
XLA Modules:
  0.0 43.2 jit_solution(17485233329330869883)
XLA Ops:
  1.3 0.0 copy-start
  1.3 1.6 %copy-done = bf16[256,4096]{1,0:T(8,128)(2,1)S(1)} copy-done((bf16[256,4096]{1,0:T(8,128)(2,1)S(1)}, bf16[256,4096]{1,0:T(8,128)(2,1)}, u32[]{:S(2)}) %copy-start) | copy-done | bytes 2097176
  2.9 0.0 copy-start.1
  2.9 1.4 %copy-done.1 = bf16[1536,512]{1,0:T(8,128)(2,1)S(1)} copy-done((bf16[1536,512]{1,0:T(8,128)(2,1)S(1)}, bf16[1536,512]{1,0:T(8,128)(2,1)}, u32[]{:S(2)}) %copy-start.1) | copy-done | bytes 1572888
  4.3 0.0 copy-start.2
  4.3 1.1 %copy-done.2 = bf16[256,1536]{1,0:T(8,128)(2,1)S(1)} copy-done((bf16[256,1536]{1,0:T(8,128)(2,1)S(1)}, bf16[256,1536]{1,0:T(8,128)(2,1)}, u32[]{:S(2)}) %copy-start.2) | copy-done | bytes 786456
  5.4 35.8 %shard_map.76 = (f32[8,128]{1,0:T(8,128)S(1)}, bf16[768,512]{1,0:T(8,128)(2,1)S(1)}, bf16[32,1536]{1,0:T(8,128)(2,1)S(1)}) custom-call(s32[1]{0:T(128)S(6)} %copy.10.counts, bf16[256,4096]{1,0:T(8,128)(2,1)S(1)} %copy-done, bf16[4096,512]{1,0:T(8,128)(2,1)} %thead_hbm.1, bf16[256,1536]{1,0:T(8,128)(2,1)S(1)} %copy-done.2, bf16[1536,512]{1,0:T(8,128)(2,1)S(1)} %copy-done.1), custom_call_target="tpu_custom_call" | custom-call | tf_op jit(solution)/shard_map/pallas_call | solution.py:241
  41.2 0.5 %slice.3 = f32[1,1]{1,0:T(1,128)} slice(f32[8,128]{1,0:T(8,128)S(1)} %get-tuple-element.6), slice={[0:1], [0:1]} | slice | bytes 8 | tf_op jit(solution)/shard_map/slice | solution.py:269
  41.7 0.9 %copy.11 = bf16[768,512]{1,0:T(8,128)(2,1)} copy(bf16[768,512]{1,0:T(8,128)(2,1)S(1)} %get-tuple-element.13) | data formatting | bytes 1572864
  42.6 0.6 %copy.12 = bf16[32,1536]{1,0:T(8,128)(2,1)} copy(bf16[32,1536]{1,0:T(8,128)(2,1)S(1)} %get-tuple-element.14) | data formatting | bytes 196608
Async XLA Ops:
  1.3 1.6 %copy-start = (bf16[256,4096]{1,0:T(8,128)(2,1)S(1)}, bf16[256,4096]{1,0:T(8,128)(2,1)}, u32[]{:S(2)}) copy-start(bf16[256,4096]{1,0:T(8,128)(2,1)} %th_hbm.1) | copy-start | bytes 6291460
  2.9 1.4 %copy-start.1 = (bf16[1536,512]{1,0:T(8,128)(2,1)S(1)}, bf16[1536,512]{1,0:T(8,128)(2,1)}, u32[]{:S(2)}) copy-start(bf16[1536,512]{1,0:T(8,128)(2,1)} %shead_hbm.1) | copy-start | bytes 4718596
  4.3 1.1 %copy-start.2 = (bf16[256,1536]{1,0:T(8,128)(2,1)S(1)}, bf16[256,1536]{1,0:T(8,128)(2,1)}, u32[]{:S(2)}) copy-start(bf16[256,1536]{1,0:T(8,128)(2,1)} %sh_hbm.1) | copy-start | bytes 2359300

commit v2 on v1

--- a/solution.py
+++ b/solution.py
@@ -72,15 +72,20 @@
 
 
 def fused(
-    n_tok, n_voc, cw, fw,
+    n_tok, n_in, n_out, cw, fw,
     counts, th_hbm, thead_hbm, sh_hbm, shead_hbm,
     loss_ref, head_ref, hid_ref,
     th, thead, sh, shead, part, precv, te_ref, se_ref, stat, ssend, srecv,
-    cnt, crecv, num, nrecv, hown, hrecv, grad, grecv, hs, hrv,
-    load_sem, p_ss, p_rs, c_ss, c_rs, h_ss, h_rs, s_ss, s_rs, g_ss, g_rs, n_ss, n_rs, d_ss, d_rs,
+    cnt, crecv, num, nrecv, hown, hrecv, grad, grecv, head_acc, hf, hs, yr, hp, zb, zr,
+    load_sem, p_ss, p_rs, c_ss, c_rs, h_ss, h_rs, s_ss, s_rs, g_ss, g_rs, n_ss, n_rs,
+    y_ss, y_rs, z_ss, z_rs,
 ):
     sect, tok, voc = lax.axis_index("sect"), lax.axis_index("tok"), lax.axis_index("vocab")
     rows, feats, width = sh.shape[0], sh.shape[1], shead.shape[1]
+    n_voc = n_in * n_out
+    inner, outer = voc % n_in, voc // n_in
+    in_peers = [(inner + d) % n_in for d in range(1, n_in)]
+    out_peers = [(outer + d) % n_out for d in range(1, n_out)]
     block, out_rows = feats // n_tok, rows // n_voc
     chunks, f_chunks, tiles = width // cw, feats // fw, rows // TILE
     other = {"sect": 1 - sect}
@@ -188,22 +193,39 @@
 
     acc = lax.fori_loop(0, tiles, finish_tile, jnp.zeros((TILE, 1), F32))
     num[...] = jnp.broadcast_to(jnp.sum(acc, axis=0, keepdims=True), num.shape)
-    g_cp, n_cp, d_cp = [], [], []
-    for i, p in enumerate(tok_peers):
-        n_cp.append(send(num, nrecv.at[i], n_ss.at[i], n_rs.at[i], {"tok": p}))
-        g_cp.append(send(grad, grecv.at[i], g_ss.at[i], g_rs.at[i], {"tok": p}))
+    g_cp, n_cp, y_cp, z_cp = [], [], [], []
     for f in range(f_chunks):
-        hs[f] = lax.dot_general(
+        term = lax.dot_general(
             grad[...], shead[f * fw:(f + 1) * fw, :], (((1,), (1,)), ((), ())),
             preferred_element_type=F32,
-        ).astype(BF16)
-        for i, p in enumerate(voc_peers):
-            at = pl.ds(pl.multiple_of(p * out_rows, out_rows), out_rows)
-            d_cp.append(
-                (f, i, send(hs.at[f, at, :], hrv.at[i, f], d_ss.at[i, f], d_rs.at[i, f], {"vocab": p}))
+        ).reshape(n_out, n_in, out_rows, fw)
+        hf[f] = term
+        hs[f] = term.astype(BF16)
+        for i, p in enumerate(in_peers):
+            y_cp.append(
+                send(hs.at[f, :, p], yr.at[i, f], y_ss.at[i, f], y_rs.at[i, f],
+                     {"vocab": outer * n_in + p})
             )
-
-    head = jnp.dot(hown[...], grad[...], preferred_element_type=F32)
+        if f == 0:
+            for i, p in enumerate(tok_peers):
+                n_cp.append(send(num, nrecv.at[i], n_ss.at[i], n_rs.at[i], {"tok": p}))
+                g_cp.append(send(grad, grecv.at[i], g_ss.at[i], g_rs.at[i], {"tok": p}))
+
+    head_acc[...] = jnp.dot(hown[...], grad[...], preferred_element_type=F32)
+    for f in range(f_chunks):
+        pair = hf[f, :, inner]
+        for i in range(n_in - 1):
+            y_cp[f * (n_in - 1) + i].wait_recv()
+            pair = pair + yr[i, f].astype(F32)
+        hp[f] = pair
+        zb[f] = pair.astype(BF16)
+        for i, p in enumerate(out_peers):
+            z_cp.append(
+                send(zb.at[f, p], zr.at[i, f], z_ss.at[i, f], z_rs.at[i, f],
+                     {"vocab": p * n_in + inner})
+            )
+
+    head = head_acc[...]
     numerator = num[...]
     for i in range(n_tok - 1):
         h_cp[i].wait_recv()
@@ -215,17 +237,13 @@
     head_ref[...] = head.astype(BF16)
     loss_ref[...] = numerator / live_total
 
-    here = pl.ds(pl.multiple_of(voc * out_rows, out_rows), out_rows)
     for f in range(f_chunks):
-        hid = hs[f, here, :].astype(F32)
-        for g, i, copy in d_cp:
-            if g == f:
-                copy.wait_recv()
-                hid = hid + hrv[i, f].astype(F32)
+        hid = hp[f, outer]
+        for i in range(n_out - 1):
+            z_cp[f * (n_out - 1) + i].wait_recv()
+            hid = hid + zr[i, f].astype(F32)
         hid_ref[:, f * fw:(f + 1) * fw] = hid.astype(BF16)
-    for copy in p_cp + c_cp + h_cp + s_cp + g_cp + n_cp:
-        copy.wait_send()
-    for _, _, copy in d_cp:
+    for copy in p_cp + c_cp + h_cp + s_cp + g_cp + n_cp + y_cp + z_cp:
         copy.wait_send()
 
 
@@ -234,12 +252,13 @@
     feats, width = student_head.shape
     cw, fw = width // 2, feats // 3
     block, out_rows = feats // n_tok, rows // n_voc
-    tp, vp, nf = n_tok - 1, n_voc - 1, feats // fw
+    n_in, n_out = 2, n_voc // 2
+    tp, vp, ip, op, nf = n_tok - 1, n_voc - 1, n_in - 1, n_out - 1, feats // fw
     vmem, dma = pltpu.VMEM, pltpu.SemaphoreType.DMA
     any_spec = pl.BlockSpec(memory_space=pl.ANY)
     vm_spec = pl.BlockSpec(memory_space=pltpu.VMEM)
     loss, head, hid = pl.pallas_call(
-        functools.partial(fused, n_tok, n_voc, cw, fw),
+        functools.partial(fused, n_tok, n_in, n_out, cw, fw),
         out_shape=(
             jax.ShapeDtypeStruct((8, 128), F32),
             jax.ShapeDtypeStruct((block, width), BF16),
@@ -257,13 +276,17 @@
             vmem((8, 128), F32), vmem((tp, 8, 128), F32),
             vmem((block, rows), BF16), vmem((tp, rows, block), BF16),
             vmem((rows, width), BF16), vmem((tp, rows, width), BF16),
-            vmem((nf, rows, fw), BF16), vmem((vp, nf, out_rows, fw), BF16),
+            vmem((block, width), F32),
+            vmem((nf, n_out, n_in, out_rows, fw), F32), vmem((nf, n_out, n_in, out_rows, fw), BF16),
+            vmem((ip, nf, n_out, out_rows, fw), BF16),
+            vmem((nf, n_out, out_rows, fw), F32), vmem((nf, n_out, out_rows, fw), BF16),
+            vmem((op, nf, out_rows, fw), BF16),
             dma((5,)), dma((4,)), dma((4,)), dma((tp,)), dma((tp,)), dma((tp,)), dma((tp,)),
             dma((vp,)), dma((vp,)), dma((tp,)), dma((tp,)), dma((tp,)), dma((tp,)),
-            dma((vp, nf)), dma((vp, nf)),
+            dma((ip, nf)), dma((ip, nf)), dma((op, nf)), dma((op, nf)),
         ],
         compiler_params=pltpu.CompilerParams(
-            collective_id=0, has_side_effects=True, vmem_limit_bytes=48 * 1024 * 1024
+            collective_id=0, has_side_effects=True, vmem_limit_bytes=60 * 1024 * 1024
         ),
     )(live_counts, teacher_hidden, teacher_head, student_hidden, student_head)
     return (loss[0, 0], head, hid)
@@ -275,7 +298,7 @@
 
     def run(*args):
         rows = args[0].shape[0]
-        if rows % (TILE * n_voc) == 0 and n_tok > 1:
+        if rows % (TILE * n_voc) == 0 and n_voc % 2 == 0 and n_voc > 2 and n_tok > 1:
             return fused_body(n_tok, n_voc, *args)
         return body(*args)
 

time: 43.5 us -> 40.2 us (0.924)
  Pallas kernels: 35.8 us -> 33.9 us
  local copies, waits for them, and re-layouts: 6.16 us -> 4.79 us
    unnamed x8 -> x2, local copies, waits for them, and re-layouts: 5.64 us -> 3.6 us
    pallas_call x1, Pallas kernels: 35.8 us -> 33.9 us  [fused_body(): pl.pallas_call(functools.partial(fused, n_tok, n_in, n_out, cw, fw), out_...]
    slice x1, local copies, waits for them, and re-layouts: 0.51 us -> 1.19 us  [fused_body(): return (loss[0, 0], head, hid)]
where the time goes in v2:
time: 40.2 us; the launch traced here: 40 us
  Pallas kernels  33.9 us (84%)
  local copies, waits for them, and re-layouts  4.79 us (12%)
  between operations  1.29 us (3%)
    pallas_call x1, Pallas kernels, fused_body(): pl.pallas_call(functools.partial(fused, n_tok, n_in, n_out, cw, fw), out_...  33.9 us
    unnamed x2, local copies, waits for them, and re-layouts  3.6 us
    slice x1, local copies, waits for them, and re-layouts, fused_body(): return (loss[0, 0], head, hid)  1.19 us

profile of v2, /device:TPU:0, one launch (start us, length us, event | category | flops | bytes accessed | tf_op | source)
XLA Modules:
  0.0 40.0 jit_solution(7591970701852318939)
XLA Ops:
  1.3 33.9 %shard_map.76 = (f32[8,128]{1,0:T(8,128)}, bf16[768,512]{1,0:T(8,128)(2,1)}, bf16[32,1536]{1,0:T(8,128)(2,1)}) custom-call(s32[1]{0:T(128)S(6)} %copy.10.counts, bf16[256,4096]{1,0:T(8,128)(2,1)} %th_hbm.1, bf16[4096,512]{1,0:T(8,128)(2,1)} %thead_hbm.1, bf16[256,1536]{1,0:T(8,128)(2,1)} %sh_hbm.1, bf16[1536,512]{1,0:T(8,128)(2,1)} %shead_hbm.1), custom_call_target="tpu_custom_call" | custom-call | tf_op jit(solution)/shard_map/pallas_call | solution.py:260
  35.2 1.2 %slice.3 = f32[1,1]{1,0:T(1,128)} slice(f32[8,128]{1,0:T(8,128)} %get-tuple-element.6), slice={[0:1], [0:1]} | slice | bytes 8 | tf_op jit(solution)/shard_map/slice | solution.py:292
  36.4 2.1 %copy.11 = bf16[768,512]{1,0:T(8,128)(2,1)} copy(bf16[768,512]{1,0:T(8,128)(2,1)} %get-tuple-element.13) | data formatting | bytes 1572864
  38.4 1.5 %copy.12 = bf16[32,1536]{1,0:T(8,128)(2,1)} copy(bf16[32,1536]{1,0:T(8,128)(2,1)} %get-tuple-element.14) | data formatting | bytes 196608

commit v3 on v2

--- a/solution.py
+++ b/solution.py
@@ -122,15 +122,16 @@
     cnt[...] = jnp.full(cnt.shape, counts[0].astype(F32))
     loads[0].wait()
     loads[1].wait()
+    for c in range(chunks):
+        part[c] = jnp.dot(sh[...], shead[:, c * cw:(c + 1) * cw], preferred_element_type=F32)
     pl.semaphore_wait(barrier, n_tok + n_voc - 1)
     c_cp, h_cp, p_cp = [], [], []
+    for c in range(chunks):
+        p_cp.append(send(part.at[c], precv.at[c], p_ss.at[c], p_rs.at[c], other))
     for i, p in enumerate(tok_peers):
         c_cp.append(send(cnt, crecv.at[i], c_ss.at[i], c_rs.at[i], {"tok": p}))
         cols = pl.ds(pl.multiple_of(p * block, block), block)
         h_cp.append(send(sh.at[:, cols], hrecv.at[i], h_ss.at[i], h_rs.at[i], {"tok": p}))
-    for c in range(chunks):
-        part[c] = jnp.dot(sh[...], shead[:, c * cw:(c + 1) * cw], preferred_element_type=F32)
-        p_cp.append(send(part.at[c], precv.at[c], p_ss.at[c], p_rs.at[c], other))
     loads[2].wait()
     for c in range(chunks):
         loads[3 + c].wait()
@@ -250,7 +251,7 @@
 def fused_body(n_tok, n_voc, teacher_hidden, teacher_head, student_hidden, student_head, live_counts):
     rows, t_feats = teacher_hidden.shape
     feats, width = student_head.shape
-    cw, fw = width // 2, feats // 3
+    cw, fw = width // 2, feats // 6
     block, out_rows = feats // n_tok, rows // n_voc
     n_in, n_out = 2, n_voc // 2
     tp, vp, ip, op, nf = n_tok - 1, n_voc - 1, n_in - 1, n_out - 1, feats // fw
@@ -286,7 +287,7 @@
             dma((ip, nf)), dma((ip, nf)), dma((op, nf)), dma((op, nf)),
         ],
         compiler_params=pltpu.CompilerParams(
-            collective_id=0, has_side_effects=True, vmem_limit_bytes=60 * 1024 * 1024
+            collective_id=0, has_side_effects=True, vmem_limit_bytes=53 * 1024 * 1024
         ),
     )(live_counts, teacher_hidden, teacher_head, student_hidden, student_head)
     return (loss[0, 0], head, hid)

time: 40.2 us -> 34.9 us (0.87)
  local copies, waits for them, and re-layouts: 4.79 us -> 2.03 us
  Pallas kernels: 33.9 us -> 31.4 us
    pallas_call x1, Pallas kernels: 33.9 us -> 31.4 us  [fused_body(): pl.pallas_call(functools.partial(fused, n_tok, n_in, n_out, cw, fw), out_...]
    unnamed x2, local copies, waits for them, and re-layouts: 3.6 us -> 1.52 us
    slice x1, local copies, waits for them, and re-layouts: 1.19 us -> 0.51 us  [fused_body(): return (loss[0, 0], head, hid)]
where the time goes in v3:
time: 34.9 us; the launch traced here: 34.7 us
  Pallas kernels  31.4 us (90%)
  local copies, waits for them, and re-layouts  2.03 us (6%)
  between operations  1.29 us (4%)
    pallas_call x1, Pallas kernels, fused_body(): pl.pallas_call(functools.partial(fused, n_tok, n_in, n_out, cw, fw), out_...  31.4 us
    unnamed x2, local copies, waits for them, and re-layouts  1.52 us

profile of v3, /device:TPU:0, one launch (start us, length us, event | category | flops | bytes accessed | tf_op | source)
XLA Modules:
  0.0 34.7 jit_solution(9630657351662914410)
XLA Ops:
  1.3 31.4 %shard_map.76 = (f32[8,128]{1,0:T(8,128)S(1)}, bf16[768,512]{1,0:T(8,128)(2,1)S(1)}, bf16[32,1536]{1,0:T(8,128)(2,1)S(1)}) custom-call(s32[1]{0:T(128)S(6)} %copy.10.counts, bf16[256,4096]{1,0:T(8,128)(2,1)} %th_hbm.1, bf16[4096,512]{1,0:T(8,128)(2,1)} %thead_hbm.1, bf16[256,1536]{1,0:T(8,128)(2,1)} %sh_hbm.1, bf16[1536,512]{1,0:T(8,128)(2,1)} %shead_hbm.1), custom_call_target="tpu_custom_call" | custom-call | tf_op jit(solution)/shard_map/pallas_call | solution.py:261
  32.7 0.5 %slice.3 = f32[1,1]{1,0:T(1,128)} slice(f32[8,128]{1,0:T(8,128)S(1)} %get-tuple-element.6), slice={[0:1], [0:1]} | slice | bytes 8 | tf_op jit(solution)/shard_map/slice | solution.py:293
  33.2 0.9 %copy.11 = bf16[768,512]{1,0:T(8,128)(2,1)} copy(bf16[768,512]{1,0:T(8,128)(2,1)S(1)} %get-tuple-element.13) | data formatting | bytes 1572864
  34.1 0.6 %copy.12 = bf16[32,1536]{1,0:T(8,128)(2,1)} copy(bf16[32,1536]{1,0:T(8,128)(2,1)S(1)} %get-tuple-element.14) | data formatting | bytes 196608

commit v4 on v3

--- a/solution.py
+++ b/solution.py
@@ -138,7 +138,6 @@
         q = chunks + c
         part[q] = jnp.dot(th[...], thead[c], preferred_element_type=F32)
         p_cp.append(send(part.at[q], precv.at[q], p_ss.at[q], p_rs.at[q], other))
-    hown[...] = sh[:, pl.ds(pl.multiple_of(tok * block, block), block)].T
     for copy in p_cp:
         copy.wait_recv()
 
@@ -165,6 +164,7 @@
         send(ssend, srecv.at[i], s_ss.at[i], s_rs.at[i], {"vocab": p})
         for i, p in enumerate(voc_peers)
     ]
+    hown[...] = sh[:, pl.ds(pl.multiple_of(tok * block, block), block)].T
     for copy in c_cp:
         copy.wait_recv()
     total = cnt[...]
@@ -212,7 +212,6 @@
                 n_cp.append(send(num, nrecv.at[i], n_ss.at[i], n_rs.at[i], {"tok": p}))
                 g_cp.append(send(grad, grecv.at[i], g_ss.at[i], g_rs.at[i], {"tok": p}))
 
-    head_acc[...] = jnp.dot(hown[...], grad[...], preferred_element_type=F32)
     for f in range(f_chunks):
         pair = hf[f, :, inner]
         for i in range(n_in - 1):
@@ -225,6 +224,8 @@
                 send(zb.at[f, p], zr.at[i, f], z_ss.at[i, f], z_rs.at[i, f],
                      {"vocab": p * n_in + inner})
             )
+        if f == f_chunks // 2:
+            head_acc[...] = jnp.dot(hown[...], grad[...], preferred_element_type=F32)
 
     head = head_acc[...]
     numerator = num[...]

time: 34.9 us -> 34.9 us (level)
  no operation moved by 1% of the time
where the time goes in v4:
time: 34.9 us; the launch traced here: 34.7 us
  Pallas kernels  31.4 us (90%)
  local copies, waits for them, and re-layouts  2.03 us (6%)
  between operations  1.29 us (4%)
    pallas_call x1, Pallas kernels, fused_body(): pl.pallas_call(functools.partial(fused, n_tok, n_in, n_out, cw, fw), out_...  31.4 us
    unnamed x2, local copies, waits for them, and re-layouts  1.52 us

profile of v4, /device:TPU:0, one launch (start us, length us, event | category | flops | bytes accessed | tf_op | source)
XLA Modules:
  0.0 34.7 jit_solution(7080226320823005434)
XLA Ops:
  1.3 31.4 %shard_map.76 = (f32[8,128]{1,0:T(8,128)S(1)}, bf16[768,512]{1,0:T(8,128)(2,1)S(1)}, bf16[32,1536]{1,0:T(8,128)(2,1)S(1)}) custom-call(s32[1]{0:T(128)S(6)} %copy.10.counts, bf16[256,4096]{1,0:T(8,128)(2,1)} %th_hbm.1, bf16[4096,512]{1,0:T(8,128)(2,1)} %thead_hbm.1, bf16[256,1536]{1,0:T(8,128)(2,1)} %sh_hbm.1, bf16[1536,512]{1,0:T(8,128)(2,1)} %shead_hbm.1), custom_call_target="tpu_custom_call" | custom-call | tf_op jit(solution)/shard_map/pallas_call | solution.py:262
  32.7 0.5 %slice.3 = f32[1,1]{1,0:T(1,128)} slice(f32[8,128]{1,0:T(8,128)S(1)} %get-tuple-element.6), slice={[0:1], [0:1]} | slice | bytes 8 | tf_op jit(solution)/shard_map/slice | solution.py:294
  33.2 0.9 %copy.11 = bf16[768,512]{1,0:T(8,128)(2,1)} copy(bf16[768,512]{1,0:T(8,128)(2,1)S(1)} %get-tuple-element.13) | data formatting | bytes 1572864
  34.1 0.6 %copy.12 = bf16[32,1536]{1,0:T(8,128)(2,1)} copy(bf16[32,1536]{1,0:T(8,128)(2,1)S(1)} %get-tuple-element.14) | data formatting | bytes 196608

commit v5 on v4

--- a/solution.py
+++ b/solution.py
@@ -247,6 +247,18 @@
         hid_ref[:, f * fw:(f + 1) * fw] = hid.astype(BF16)
     for copy in p_cp + c_cp + h_cp + s_cp + g_cp + n_cp + y_cp + z_cp:
         copy.wait_send()
+
+
+def emit(loss_in, head_in, hid_in, loss_out, head_out, hid_out, sems):
+    copies = [
+        pltpu.make_async_copy(head_in, head_out, sems.at[0]),
+        pltpu.make_async_copy(hid_in, hid_out, sems.at[1]),
+    ]
+    for copy in copies:
+        copy.start()
+    loss_out[...] = loss_in[0:1, 0:1]
+    for copy in copies:
+        copy.wait()
 
 
 def fused_body(n_tok, n_voc, teacher_hidden, teacher_head, student_hidden, student_head, live_counts):
@@ -291,6 +303,18 @@
             collective_id=0, has_side_effects=True, vmem_limit_bytes=53 * 1024 * 1024
         ),
     )(live_counts, teacher_hidden, teacher_head, student_hidden, student_head)
+    loss, head, hid = pl.pallas_call(
+        emit,
+        out_shape=(
+            jax.ShapeDtypeStruct((1, 1), F32),
+            jax.ShapeDtypeStruct(head.shape, BF16),
+            jax.ShapeDtypeStruct(hid.shape, BF16),
+        ),
+        in_specs=[vm_spec, any_spec, any_spec],
+        out_specs=(vm_spec, any_spec, any_spec),
+        scratch_shapes=[dma((2,))],
+        compiler_params=pltpu.CompilerParams(vmem_limit_bytes=4 * 1024 * 1024),
+    )(loss, head, hid)
     return (loss[0, 0], head, hid)
 
 

time: 34.9 us -> 34.3 us (0.983)
  local copies, waits for them, and re-layouts: 2.03 us -> 0 us
  Pallas kernels: 31.4 us -> 32.8 us
    unnamed x2 -> x0, local copies, waits for them, and re-layouts: 1.52 us -> none
    pallas_call x0 -> x1, Pallas kernels: none -> 1.43 us  [fused_body(): pl.pallas_call(emit, out_shape=(jax.ShapeDtypeStruct((1, 1), F32), jax.Sh...]
    slice x1 -> x0, local copies, waits for them, and re-layouts: 0.51 us -> none  [fused_body(): return (loss[0, 0], head, hid)]
where the time goes in v5:
time: 34.3 us; the launch traced here: 34.1 us
  Pallas kernels  32.8 us (96%)
  between operations  1.29 us (4%)
    pallas_call x1, Pallas kernels, fused_body(): pl.pallas_call(functools.partial(fused, n_tok, n_in, n_out, cw, fw), out_...  31.4 us
    pallas_call x1, Pallas kernels, fused_body(): pl.pallas_call(emit, out_shape=(jax.ShapeDtypeStruct((1, 1), F32), jax.Sh...  1.43 us

profile of v5, /device:TPU:0, one launch (start us, length us, event | category | flops | bytes accessed | tf_op | source)
XLA Modules:
  0.0 34.1 jit_solution(8804887642151746716)
XLA Ops:
  1.3 31.4 %shard_map.76 = (f32[8,128]{1,0:T(8,128)S(1)}, bf16[768,512]{1,0:T(8,128)(2,1)S(1)}, bf16[32,1536]{1,0:T(8,128)(2,1)S(1)}) custom-call(s32[1]{0:T(128)S(6)} %copy.8.counts, bf16[256,4096]{1,0:T(8,128)(2,1)} %th_hbm.1, bf16[4096,512]{1,0:T(8,128)(2,1)} %thead_hbm.1, bf16[256,1536]{1,0:T(8,128)(2,1)} %sh_hbm.1, bf16[1536,512]{1,0:T(8,128)(2,1)} %shead_hbm.1), custom_call_target="tpu_custom_call" | custom-call | tf_op jit(solution)/shard_map/pallas_call | solution.py:274
  32.7 1.4 %shard_map.77 = (f32[1,1]{1,0:T(1,128)}, bf16[768,512]{1,0:T(8,128)(2,1)}, bf16[32,1536]{1,0:T(8,128)(2,1)}) custom-call(f32[8,128]{1,0:T(8,128)S(1)} %get-tuple-element.9.loss_in, bf16[768,512]{1,0:T(8,128)(2,1)S(1)} %get-tuple-element.10.head_in, bf16[32,1536]{1,0:T(8,128)(2,1)S(1)} %get-tuple-element.11.hid_in), custom_call_target="tpu_custom_call" | custom-call | tf_op jit(solution)/shard_map/pallas_call | solution.py:306

commit v6 on v5

--- a/solution.py
+++ b/solution.py
@@ -250,9 +250,12 @@
 
 
 def emit(loss_in, head_in, hid_in, loss_out, head_out, hid_out, sems):
-    copies = [
-        pltpu.make_async_copy(head_in, head_out, sems.at[0]),
-        pltpu.make_async_copy(hid_in, hid_out, sems.at[1]),
+    piece = head_in.shape[0] // 4
+    copies = [pltpu.make_async_copy(hid_in, hid_out, sems.at[4])] + [
+        pltpu.make_async_copy(
+            head_in.at[pl.ds(i * piece, piece)], head_out.at[pl.ds(i * piece, piece)], sems.at[i]
+        )
+        for i in range(4)
     ]
     for copy in copies:
         copy.start()
@@ -312,7 +315,7 @@
         ),
         in_specs=[vm_spec, any_spec, any_spec],
         out_specs=(vm_spec, any_spec, any_spec),
-        scratch_shapes=[dma((2,))],
+        scratch_shapes=[dma((5,))],
         compiler_params=pltpu.CompilerParams(vmem_limit_bytes=4 * 1024 * 1024),
     )(loss, head, hid)
     return (loss[0, 0], head, hid)

time: 34.3 us -> 34.3 us (level)
  no operation moved by 1% of the time
where the time goes in v6:
time: 34.3 us; the launch traced here: 34.1 us
  Pallas kernels  32.9 us (96%)
  between operations  1.29 us (4%)
    pallas_call x1, Pallas kernels, fused_body(): pl.pallas_call(functools.partial(fused, n_tok, n_in, n_out, cw, fw), out_...  31.4 us
    pallas_call x1, Pallas kernels, fused_body(): pl.pallas_call(emit, out_shape=(jax.ShapeDtypeStruct((1, 1), F32), jax.Sh...  1.46 us

profile of v6, /device:TPU:0, one launch (start us, length us, event | category | flops | bytes accessed | tf_op | source)
XLA Modules:
  0.0 34.1 jit_solution(671530985587356686)
XLA Ops:
  1.3 31.4 %shard_map.76 = (f32[8,128]{1,0:T(8,128)S(1)}, bf16[768,512]{1,0:T(8,128)(2,1)S(1)}, bf16[32,1536]{1,0:T(8,128)(2,1)S(1)}) custom-call(s32[1]{0:T(128)S(6)} %copy.8.counts, bf16[256,4096]{1,0:T(8,128)(2,1)} %th_hbm.1, bf16[4096,512]{1,0:T(8,128)(2,1)} %thead_hbm.1, bf16[256,1536]{1,0:T(8,128)(2,1)} %sh_hbm.1, bf16[1536,512]{1,0:T(8,128)(2,1)} %shead_hbm.1), custom_call_target="tpu_custom_call" | custom-call | tf_op jit(solution)/shard_map/pallas_call | solution.py:277
  32.7 1.5 %shard_map.77 = (f32[1,1]{1,0:T(1,128)}, bf16[768,512]{1,0:T(8,128)(2,1)}, bf16[32,1536]{1,0:T(8,128)(2,1)}) custom-call(f32[8,128]{1,0:T(8,128)S(1)} %get-tuple-element.9.loss_in, bf16[768,512]{1,0:T(8,128)(2,1)S(1)} %get-tuple-element.10.head_in, bf16[32,1536]{1,0:T(8,128)(2,1)S(1)} %get-tuple-element.11.hid_in), custom_call_target="tpu_custom_call" | custom-call | tf_op jit(solution)/shard_map/pallas_call | solution.py:309
